TPU v7x, 32 devices: a whole 2x2x4 slice. The times are simulated.
32 devices in a mesh: node: 8 (over z, core), local: 4 (over y, x).
Axes of the slice: x: 2, y: 2, z: 4, core: 2. Of those that a mesh axis runs over, the one named last changes fastest.
Arguments:
- tokens: bfloat16 [64, 7168], P(('node', 'local')), may hold values from -6 to 6
- expert_ids: int32 [64, 8], P(('node', 'local')), may hold values from 0 to 31, all different within a row; in each aligned block of 8 rows (0 to 7, 8 to 15, ...) at most 4 rows name the same one
- gate_weights: bfloat16 [64, 8], P(('node', 'local')), may hold values from 0.049804688 to 1
- expert_seeds: int32 [32], P('node'), may hold values from 0 to 16777215
Outputs:
- moe_out: bfloat16 [64, 7168], P(('node', 'local'))
Inputs may be any that keep to these rules, and one draw needn't show every extreme that they name: `expert_ids`: each row names 8 different experts. Within the tokens of one node group (aligned blocks of 8 rows), no expert is named by more than 4 rows, a bound that some block reaches.
All inputs are finite; a program needn't handle non-finite values.
Results may differ from a plain program's by a relative error of at most 0.0078.
Values may be sent and summed in bfloat16 or wider, within the bound.
No kernel may reach another device: no remote copies, remote signals or barrier semaphores. Data moves between devices by JAX's collectives and lax.ppermute only.
A program may use at most 128 MiB of HBM per device.

v0:
```python
import math

import jax
import jax.numpy as jnp
from jax import lax
from jax.sharding import PartitionSpec as P

FF = 2048
TOP = 8
EXP_NODE = 4


mix_const = 73244475


def hashed_weights(expert_seed, matrix_code, row_ids, col_ids, col_count, fan_in):
    flat_index = row_ids[:, None] * col_count + col_ids[None, :]
    mixing = expert_seed + matrix_code * 1000003 + flat_index * 374761393
    mixing = mixing ^ jnp.right_shift(mixing, 16)
    mixing = mixing * mix_const
    mixing = mixing ^ jnp.right_shift(mixing, 15)
    mixing = mixing * mix_const
    mixing = mixing ^ jnp.right_shift(mixing, 16)
    uniform_part = (mixing & 16777215).astype(jnp.float32) * (1.0 / 16777216.0) - 0.5
    return (uniform_part * math.sqrt(12.0 / fan_in)).astype(jnp.bfloat16)


def block_weights(expert_seed, hidden_ids, model_width, hidden_total):
    feature_ids = jnp.arange(model_width, dtype=jnp.int32)
    gate_and_up = jnp.concatenate(
        [
            hashed_weights(expert_seed, 0, feature_ids, hidden_ids, hidden_total, model_width),
            hashed_weights(expert_seed, 1, feature_ids, hidden_ids, hidden_total, model_width),
        ],
        axis=1,
    )
    w_down = hashed_weights(expert_seed, 2, hidden_ids, feature_ids, model_width, hidden_total)
    return (gate_and_up, w_down)


def apply_block(row_block, gate_and_up, w_down):
    hidden_block = w_down.shape[0]
    projected = jnp.dot(row_block, gate_and_up, preferred_element_type=jnp.float32)
    hidden = (jax.nn.silu(projected[:, :hidden_block]) * projected[:, hidden_block:]).astype(
        jnp.bfloat16
    )
    return jnp.dot(hidden, w_down, preferred_element_type=jnp.float32)


def quarter_output(flat_rows, expert_seed, first_unit, quarter_width, hidden_block):
    model_width = flat_rows.shape[1]
    accumulated = jnp.zeros((flat_rows.shape[0], model_width), jnp.float32)
    for offset in range(0, quarter_width, hidden_block):
        hidden_ids = first_unit + offset + jnp.arange(hidden_block, dtype=jnp.int32)
        gate_and_up, w_down = block_weights(expert_seed, hidden_ids, model_width, FF)
        accumulated = accumulated + apply_block(flat_rows, gate_and_up, w_down)
    return accumulated.astype(jnp.bfloat16)


def body(tokens, expert_ids, gate_weights, expert_seeds):
    n_node = lax.axis_size("node")
    n_local = lax.axis_size("local")
    quarters = n_local // EXP_NODE
    quarter_width = FF // quarters
    hidden_block = min(quarter_width, 256)
    model_width = tokens.shape[1]
    group_rows, group_ids, group_gates = (
        lax.all_gather(tokens, "local", axis=0, tiled=True),
        lax.all_gather(expert_ids, "local", axis=0, tiled=True),
        lax.all_gather(gate_weights, "local", axis=0, tiled=True),
    )
    tok_node = group_rows.shape[0]
    capacity = 2 * tok_node * TOP // (EXP_NODE * n_node)
    local_index = lax.axis_index("local")
    expert_kind = local_index // quarters
    quarter = local_index % quarters
    targets = (
        jnp.arange(n_node, dtype=jnp.int32)[:, None] * EXP_NODE
        + jnp.arange(EXP_NODE, dtype=jnp.int32)[None, :]
    )
    id_match = group_ids[:, :, None, None] == targets[None, None, :, :]
    routed_hits = jnp.any(id_match, axis=1)
    picked = jnp.sum(
        jnp.where(id_match, group_gates.astype(jnp.float32)[:, :, None, None], 0.0), axis=1
    )
    counts = jnp.cumsum(routed_hits.astype(jnp.int32), axis=0) - 1
    slot_place = jnp.where(routed_hits, counts, -1)
    slot_select = (
        jnp.transpose(slot_place, (1, 2, 0))[:, :, None, :]
        == jnp.arange(capacity, dtype=jnp.int32)[None, None, :, None]
    )
    expert_seed = expert_seeds[expert_kind]
    first_unit = quarter * quarter_width
    own_select = lax.dynamic_index_in_dim(slot_select, expert_kind, 1, keepdims=False)
    own_picked = lax.dynamic_index_in_dim(picked, expert_kind, 2, keepdims=False)
    outgoing = jnp.einsum(
        "mct,td->mcd",
        own_select.astype(jnp.bfloat16),
        group_rows,
        preferred_element_type=jnp.float32,
    ).astype(jnp.bfloat16)
    arrived = lax.all_to_all(outgoing, "node", split_axis=0, concat_axis=0, tiled=True)
    row_total = arrived.shape[0] * arrived.shape[1]
    flat_rows = arrived.reshape(row_total, model_width)
    flat_out = quarter_output(flat_rows, expert_seed, first_unit, quarter_width, hidden_block)
    returned = lax.all_to_all(
        flat_out.reshape(arrived.shape), "node", split_axis=0, concat_axis=0, tiled=True
    )
    combine_weights = own_select.astype(jnp.float32) * own_picked.T[:, None, :]
    partial_term = jnp.einsum(
        "mct,mcd->td",
        combine_weights,
        returned.astype(jnp.float32),
        precision=lax.Precision.HIGHEST,
    )
    own_rows = lax.psum_scatter(partial_term, "local", scatter_dimension=0, tiled=True)
    return own_rows.astype(jnp.bfloat16)


def solution(mesh):
    return jax.shard_map(
        body,
        mesh=mesh,
        in_specs=(
            P(("node", "local"), None),
            P(("node", "local"), None),
            P(("node", "local"), None),
            P("node"),
        ),
        out_specs=P(("node", "local"), None),
        check_vma=False,
    )
```

profile of v0, /device:TPU:0, one launch (start us, length us, event | category | flops | bytes accessed | tf_op | source)
XLA Modules:
  0.0 199.2 jit_solution(6134852472920081447)
XLA Ops:
  0.0 10.1 %all-gather.2 = bf16[4,2,7168]{2,1,0:T(2,128)(2,1)S(1)} all-gather(bf16[1,2,7168]{2,1,0:T(2,128)(2,1)} %bitcast.32), channel_id=1, replica_groups=mesh['node'=8,'local'=4] {'local'}, dimensions={0}, use_global_device_ids=true | all-gather | bytes 143360 | tf_op jit(solution)/shard_map/all_gather | solution.py:68
  10.2 7.9 %all-gather = s32[4,2,8]{2,1,0:T(2,128)S(1)} all-gather(s32[1,2,8]{2,1,0:T(2,128)} %bitcast.35), channel_id=1, replica_groups=mesh['node'=8,'local'=4] {'local'}, dimensions={0}, use_global_device_ids=true | all-gather | bytes 320 | tf_op jit(solution)/shard_map/all_gather | solution.py:69
  18.6 1.1 copy.18
  19.7 4.9 %all-to-all-start = ((bf16[8,4,7168]{2,1,0:T(4,128)(2,1)}), bf16[8,4,7168]{2,1,0:T(4,128)(2,1)S(1)}, u32[]{:S(2)}, u32[]{:S(2)}) async-start(bf16[8,4,7168]{2,1,0:T(4,128)(2,1)} %copy.18), calls=%async_computation | async-start | bytes 917504 | tf_op jit(solution)/shard_map/all_to_all | solution.py:102
  24.6 1.2 dynamic_slice.13
  26.5 69.3 %fusion.176 = (bf16[7168,256]{1,0:T(8,128)(2,1)}, bf16[7168,256]{1,0:T(8,128)(2,1)}, bf16[7168,256]{1,0:T(8,128)(2,1)}, bf16[7168,256]{1,0:T(8,128)(2,1)}, bf16[...) fusion(s32[256]{0:T(256)S(1)} %get-tuple-element.33, ...), kind=kLoop, calls=%fused_computation.257 | loop fusion | flops 469762048 | bytes 58756104 | tf_op jit(solution)/shard_map/convert_element_type | solution.py:25
  96.7 4.2 %fusion.193 = f32[32,512]{1,0:T(8,128)S(1)} fusion(bf16[32,7168]{1,0:T(8,128)(2,1)S(1)} %reshape.115, bf16[7168,256]{1,0:T(8,128)(2,1)} %get-tuple-element.31, bf16[7168,256]{1,0:T(8,128)(2,1)} %get-tuple-element.32), kind=kOutput, calls=%fused_computation.274 | convolution fusion | flops 249561088 | bytes 7864320 | tf_op jit(solution)/shard_map/dot_general | solution.py:43
  102.1 1.3 fusion.197
  104.1 1.1 copy-done.11
  105.2 1.3 fusion.201
  107.3 1.1 copy-done.9
  108.4 1.3 fusion.205
  110.4 1.1 copy-done.7
  111.5 1.3 fusion.209
  113.6 1.1 copy-done.5
  114.7 1.3 fusion.213
  116.7 1.1 copy-done.3
  117.8 1.3 fusion.217
  119.9 1.1 copy-done.1
  121.0 1.3 fusion.221
  122.3 4.4 %fusion.302 = f32[32,7168]{1,0:T(8,128)S(1)} fusion(s32[256]{0:T(256)S(1)} %iota_multiply_fusion.1, s32[]{:T(128)S(6)} %add.686, f32[32,512]{1,0:T(8,128)S(1)} %fusion.193), kind=kOutput, calls=%fused_computation.384 | convolution fusion | flops 148684800 | bytes 984068 | tf_op jit(solution)/shard_map/dot_general | solution.py:47
  126.8 4.7 %convolution_add_fusion.6 = f32[32,7168]{1,0:T(8,128)S(1)} fusion(f32[32,7168]{1,0:T(8,128)S(1)} %fusion.302, s32[256]{0:T(256)S(1)} %broadcast_multiply_fusion.6, s32[]{:T(128)S(6)} %add.686, f32[32,512]{1,0:T(8,128)S(1)} %fusion.197), kind=kOutput, calls=%fused_computation.78 | convolution fusion | flops 148914176 | bytes 1901572 | tf_op jit(solution)/shard_map/dot_general | solution.py:47
  131.4 4.4 %convolution_add_fusion.5 = f32[32,7168]{1,0:T(8,128)S(1)} fusion(f32[32,7168]{1,0:T(8,128)S(1)} %convolution_add_fusion.6, s32[256]{0:T(256)S(1)} %broadcast_multiply_fusion.5, s32[]{:T(128)S(6)} %add.686, f32[32,512]{1,0:T(8,128)S(1)} %fusion.201), kind=kOutput, calls=%fused_computation.77 | convolution fusion | flops 148914176 | bytes 1901572 | tf_op jit(solution)/shard_map/dot_general | solution.py:47
  135.9 4.4 %convolution_add_fusion.4 = f32[32,7168]{1,0:T(8,128)S(1)} fusion(f32[32,7168]{1,0:T(8,128)S(1)} %convolution_add_fusion.5, s32[256]{0:T(256)S(1)} %broadcast_multiply_fusion.4, s32[]{:T(128)S(6)} %add.686, f32[32,512]{1,0:T(8,128)S(1)} %fusion.205), kind=kOutput, calls=%fused_computation.76 | convolution fusion | flops 148914176 | bytes 1901572 | tf_op jit(solution)/shard_map/dot_general | solution.py:47
  140.3 4.8 %convolution_add_fusion.3 = f32[32,7168]{1,0:T(8,128)S(1)} fusion(f32[32,7168]{1,0:T(8,128)S(1)} %convolution_add_fusion.4, s32[256]{0:T(256)S(1)} %broadcast_multiply_fusion.3, s32[]{:T(128)S(6)} %add.686, f32[32,512]{1,0:T(8,128)S(1)} %fusion.209), kind=kOutput, calls=%fused_computation.75 | convolution fusion | flops 148914176 | bytes 1901572 | tf_op jit(solution)/shard_map/dot_general | solution.py:47
  145.2 4.4 %convolution_add_fusion.2 = f32[32,7168]{1,0:T(8,128)S(1)} fusion(f32[32,7168]{1,0:T(8,128)S(1)} %convolution_add_fusion.3, s32[256]{0:T(256)S(1)} %broadcast_multiply_fusion.2, s32[]{:T(128)S(6)} %add.686, f32[32,512]{1,0:T(8,128)S(1)} %fusion.213), kind=kOutput, calls=%fused_computation.74 | convolution fusion | flops 148914176 | bytes 1901572 | tf_op jit(solution)/shard_map/dot_general | solution.py:47
  149.6 4.6 %convolution_add_fusion.1 = f32[32,7168]{1,0:T(8,128)S(1)} fusion(f32[32,7168]{1,0:T(8,128)S(1)} %convolution_add_fusion.2, s32[256]{0:T(256)S(1)} %broadcast_multiply_fusion.1, s32[]{:T(128)S(6)} %add.686, f32[32,512]{1,0:T(8,128)S(1)} %fusion.217), kind=kOutput, calls=%fused_computation.73 | convolution fusion | flops 148914176 | bytes 1901572 | tf_op jit(solution)/shard_map/dot_general | solution.py:47
  154.3 4.5 %fusion = bf16[32,7168]{1,0:T(8,128)(2,1)S(1)} fusion(f32[32,7168]{1,0:T(8,128)S(1)} %convolution_add_fusion.1, s32[256]{0:T(256)S(1)} %broadcast_multiply_fusion, s32[]{:T(128)S(6)} %add.686, f32[32,512]{1,0:T(8,128)S(1)} %fusion.221), kind=kOutput, calls=%fused_computation.79 | convolution fusion | flops 149143552 | bytes 1442820 | tf_op jit(solution)/shard_map/dot_general | solution.py:47
  159.7 5.1 %all-to-all-start.1 = ((bf16[8,4,7168]{2,1,0:T(4,128)(2,1)}), bf16[8,4,7168]{2,1,0:T(4,128)(2,1)S(1)}, u32[]{:S(2)}, u32[]{:S(2)}) async-start(bf16[8,4,7168]{2,1,0:T(4,128)(2,1)} %reshape.116), calls=%async_computation.1 | async-start | bytes 917504 | tf_op jit(solution)/shard_map/all_to_all | solution.py:106
  164.8 7.2 %all-gather.1 = bf16[4,2,8]{2,1,0:T(2,128)(2,1)S(1)} all-gather(bf16[1,2,8]{2,1,0:T(2,128)(2,1)S(1)} %bitcast.36), channel_id=1, replica_groups=mesh['node'=8,'local'=4] {'local'}, dimensions={0}, use_global_device_ids=true | all-gather | bytes 160 | tf_op jit(solution)/shard_map/all_gather | solution.py:70
  173.4 5.3 %all-to-all-done.1 = bf16[8,4,7168]{2,1,0:T(4,128)(2,1)S(1)} async-done(((bf16[8,4,7168]{2,1,0:T(4,128)(2,1)}), bf16[8,4,7168]{2,1,0:T(4,128)(2,1)S(1)}, u32[]{:S(2)}, u32[]{:S(2)}) %all-to-all-start.1) | async-done | bytes 458784 | tf_op jit(solution)/shard_map/all_to_all | solution.py:106
  179.1 19.3 %all-reduce.2 = bf16[8,7168]{1,0:T(8,128)(2,1)S(1)} all-reduce(f32[8,7168]{1,0:T(8,128)S(1)} %convolution_bitcast_fusion), channel_id=2, replica_groups=mesh['node'=8,'local'=4] {'local'}, use_global_device_ids=true, to_apply=%region_3.4.clone | all-reduce | flops 57344 | bytes 344064
  (57 shorter events, 8.7 us)
Async XLA Ops:
  19.7 76.9 %all-to-all-start = ((bf16[8,4,7168]{2,1,0:T(4,128)(2,1)}), bf16[8,4,7168]{2,1,0:T(4,128)(2,1)S(1)}, u32[]{:S(2)}, u32[]{:S(2)}) async-start(bf16[8,4,7168]{2,1,0:T(4,128)(2,1)} %copy.18), calls=%async_computation | async-start | bytes 917504 | tf_op jit(solution)/shard_map/all_to_all | solution.py:102
  96.7 4.2 %copy-start.12 = (bf16[7168,256]{1,0:T(8,128)(2,1)S(1)}, bf16[7168,256]{1,0:T(8,128)(2,1)}, u32[]{:S(2)}) copy-start(bf16[7168,256]{1,0:T(8,128)(2,1)} %get-tuple-element.19) | copy-start | bytes 11010052
  96.7 5.3 %copy-start.13 = (bf16[7168,256]{1,0:T(8,128)(2,1)S(1)}, bf16[7168,256]{1,0:T(8,128)(2,1)}, u32[]{:S(2)}) copy-start(bf16[7168,256]{1,0:T(8,128)(2,1)} %get-tuple-element.20) | copy-start | bytes 11010052
  102.1 2.0 %copy-start.10 = (bf16[7168,256]{1,0:T(8,128)(2,1)S(1)}, bf16[7168,256]{1,0:T(8,128)(2,1)}, u32[]{:S(2)}) copy-start(bf16[7168,256]{1,0:T(8,128)(2,1)} %get-tuple-element.21) | copy-start | bytes 11010052
  102.1 3.2 %copy-start.11 = (bf16[7168,256]{1,0:T(8,128)(2,1)S(1)}, bf16[7168,256]{1,0:T(8,128)(2,1)}, u32[]{:S(2)}) copy-start(bf16[7168,256]{1,0:T(8,128)(2,1)} %get-tuple-element.22) | copy-start | bytes 11010052
  105.2 2.0 %copy-start.8 = (bf16[7168,256]{1,0:T(8,128)(2,1)S(1)}, bf16[7168,256]{1,0:T(8,128)(2,1)}, u32[]{:S(2)}) copy-start(bf16[7168,256]{1,0:T(8,128)(2,1)} %get-tuple-element.23) | copy-start | bytes 11010052
  105.2 3.2 %copy-start.9 = (bf16[7168,256]{1,0:T(8,128)(2,1)S(1)}, bf16[7168,256]{1,0:T(8,128)(2,1)}, u32[]{:S(2)}) copy-start(bf16[7168,256]{1,0:T(8,128)(2,1)} %get-tuple-element.24) | copy-start | bytes 11010052
  108.4 2.0 %copy-start.6 = (bf16[7168,256]{1,0:T(8,128)(2,1)S(1)}, bf16[7168,256]{1,0:T(8,128)(2,1)}, u32[]{:S(2)}) copy-start(bf16[7168,256]{1,0:T(8,128)(2,1)} %get-tuple-element.25) | copy-start | bytes 11010052
  108.4 3.2 %copy-start.7 = (bf16[7168,256]{1,0:T(8,128)(2,1)S(1)}, bf16[7168,256]{1,0:T(8,128)(2,1)}, u32[]{:S(2)}) copy-start(bf16[7168,256]{1,0:T(8,128)(2,1)} %get-tuple-element.26) | copy-start | bytes 11010052
  111.5 2.0 %copy-start.4 = (bf16[7168,256]{1,0:T(8,128)(2,1)S(1)}, bf16[7168,256]{1,0:T(8,128)(2,1)}, u32[]{:S(2)}) copy-start(bf16[7168,256]{1,0:T(8,128)(2,1)} %get-tuple-element.27) | copy-start | bytes 11010052
  111.5 3.2 %copy-start.5 = (bf16[7168,256]{1,0:T(8,128)(2,1)S(1)}, bf16[7168,256]{1,0:T(8,128)(2,1)}, u32[]{:S(2)}) copy-start(bf16[7168,256]{1,0:T(8,128)(2,1)} %get-tuple-element.28) | copy-start | bytes 11010052
  114.7 2.0 %copy-start.2 = (bf16[7168,256]{1,0:T(8,128)(2,1)S(1)}, bf16[7168,256]{1,0:T(8,128)(2,1)}, u32[]{:S(2)}) copy-start(bf16[7168,256]{1,0:T(8,128)(2,1)} %get-tuple-element.29) | copy-start | bytes 11010052
  114.7 3.2 %copy-start.3 = (bf16[7168,256]{1,0:T(8,128)(2,1)S(1)}, bf16[7168,256]{1,0:T(8,128)(2,1)}, u32[]{:S(2)}) copy-start(bf16[7168,256]{1,0:T(8,128)(2,1)} %get-tuple-element.30) | copy-start | bytes 11010052
  117.8 2.0 %copy-start = (bf16[7168,256]{1,0:T(8,128)(2,1)S(1)}, bf16[7168,256]{1,0:T(8,128)(2,1)}, u32[]{:S(2)}) copy-start(bf16[7168,256]{1,0:T(8,128)(2,1)} %get-tuple-element.5) | copy-start | bytes 11010052
  117.8 3.2 %copy-start.1 = (bf16[7168,256]{1,0:T(8,128)(2,1)S(1)}, bf16[7168,256]{1,0:T(8,128)(2,1)}, u32[]{:S(2)}) copy-start(bf16[7168,256]{1,0:T(8,128)(2,1)} %get-tuple-element.6) | copy-start | bytes 11010052
  154.2 10.5 %copy-start.14 = (bf16[2,8]{1,0:T(2,128)(2,1)S(1)}, bf16[2,8]{1,0:T(2,128)(2,1)}, u32[]{:S(2)}) copy-start(bf16[2,8]{1,0:T(2,128)(2,1)} %param.6) | copy-start | bytes 100
  154.2 17.9 %copy-start.15 = (u32[32]{0:T(128)S(1)}, u32[32]{0:T(128)}, u32[]{:S(2)}) copy-start(u32[32]{0:T(128)} %constant.137) | copy-start | bytes 388
  159.7 19.0 %all-to-all-start.1 = ((bf16[8,4,7168]{2,1,0:T(4,128)(2,1)}), bf16[8,4,7168]{2,1,0:T(4,128)(2,1)S(1)}, u32[]{:S(2)}, u32[]{:S(2)}) async-start(bf16[8,4,7168]{2,1,0:T(4,128)(2,1)} %reshape.116), calls=%async_computation.1 | async-start | bytes 917504 | tf_op jit(solution)/shard_map/all_to_all | solution.py:106
where the time goes:
time: 203 us; the launch traced here: 199 us
  other arithmetic  69.7 us (34%)
  matrix products  50.6 us (25%)
  blocking collectives  44.5 us (22%)
  local copies, waits for them, and re-layouts  16.9 us (8%)
  starting transfers between devices  9.96 us (5%)
  waiting for transfers between devices  5.28 us (3%)
  between operations  2.37 us (1%)
    convert_element_type x1, other arithmetic, hashed_weights(): return (uniform_part * math.sqrt(12.0 / fan_in)).astype(jnp.bfloat16)  69.3 us
    dot_general x8, matrix products, apply_block(): return jnp.dot(hidden, w_down, preferred_element_type=jnp.float32)  36.4 us
    unnamed x1, blocking collectives  19.3 us
    dot_general x8, matrix products, apply_block(): jnp.dot(row_block, gate_and_up, preferred_element_type=jnp.float32)  13.6 us
    unnamed x34, local copies, waits for them, and re-layouts  12.6 us
    all_gather x1, blocking collectives, body(): lax.all_gather(tokens, 'local', axis=0, tiled=True)  10.1 us
    all_gather x1, blocking collectives, body(): lax.all_gather(expert_ids, 'local', axis=0, tiled=True)  7.86 us
    all_gather x1, blocking collectives, body(): lax.all_gather(gate_weights, 'local', axis=0, tiled=True)  7.18 us
  transfers between devices with their start and end apart: 2, of which 1 were waited for; matrix products, arithmetic and copies ran while one was open for 36% of the time, Pallas kernels for 0%

commit v1 on v0

v1 whole, which is shorter than its diff:
```python
import math

import jax
import jax.numpy as jnp
from jax import lax
from jax.experimental import pallas as pl
from jax.experimental.pallas import tpu as pltpu
from jax.sharding import PartitionSpec as P

FF = 2048
TOP = 8
EXP_NODE = 4

STEP = 374761393
MIX = 73244475
CODE = 1000003
LANES = 128
BLOCK = 256
HALF = float(1 << 23)


def wrap(value):
    value &= 0xFFFFFFFF
    return value - (1 << 32) if value >= 1 << 31 else value


def mixed(v):
    v = v ^ (v >> 16)
    v = v * MIX
    v = v ^ (v >> 15)
    v = v * MIX
    v = v ^ (v >> 16)
    return (v & 16777215).astype(jnp.float32).astype(jnp.bfloat16)


def index_table(t_ref, row_stride):
    row = lax.broadcasted_iota(jnp.int32, t_ref.shape, 0)
    col = lax.broadcasted_iota(jnp.int32, t_ref.shape, 1)
    t_ref[...] = (row * row_stride + col) * STEP


def gate_up_tile(w_ref, table, base, rows, row_stride):
    for r in range(0, rows, 16):
        for c in range(2):
            word = table + (base + wrap(r * row_stride * STEP + c * CODE))
            w_ref[r : r + 16, c * BLOCK : (c + 1) * BLOCK] = mixed(word)


def down_tile(w_ref, table, bases, first_row, rows, source_rows, row_stride):
    for r in range(0, rows, 16):
        source, unit = divmod(first_row + r, source_rows)
        word = table + (bases[source] + wrap(unit * row_stride * STEP))
        w_ref[r : r + 16, :] = mixed(word)


def params(vmem=60 << 20):
    return pltpu.CompilerParams(vmem_limit_bytes=vmem)


def smem():
    return pl.BlockSpec(memory_space=pltpu.SMEM)


def estimate(elements, rows):
    return pl.CostEstimate(flops=40 * elements + 2 * rows * elements, bytes_accessed=2 * elements, transcendentals=0)


def early_gate_up(scalars, pre_rows, blocks, hidden_total):
    half = pre_rows // 2

    def kernel(s_ref, w_ref, t_ref):
        block, part = pl.program_id(0), pl.program_id(1)
        index_table(t_ref, hidden_total)
        base = s_ref[0] + (s_ref[1] + block * BLOCK + part * (half * hidden_total)) * STEP
        gate_up_tile(w_ref.at[0], t_ref[...], base, half, hidden_total)

    return pl.pallas_call(
        kernel,
        grid=(blocks, 2),
        in_specs=[smem()],
        out_specs=pl.BlockSpec((1, half, 2 * BLOCK), lambda b, p: (b, p, 0)),
        out_shape=jax.ShapeDtypeStruct((blocks, pre_rows, 2 * BLOCK), jnp.bfloat16),
        scratch_shapes=[pltpu.VMEM((16, BLOCK), jnp.int32)],
        compiler_params=params(),
        cost_estimate=estimate(blocks * pre_rows * 2 * BLOCK, 0),
        name="early_gate_up",
    )(scalars)


def hidden_rows(scalars, rows, row_weight, early, model_width, hidden_total):
    blocks, pre_rows, _ = early.shape
    count = rows.shape[0]
    half = (model_width - pre_rows) // 2
    scale = math.sqrt(12.0 / model_width) / 16777216.0

    def kernel(s_ref, x_ref, g_ref, early_ref, h_ref, t_ref, wa, wb, shift_ref):
        block = pl.program_id(0)

        def make(step, first_row, w_ref):
            base = s_ref[0] + (s_ref[1] + step * BLOCK + first_row * hidden_total) * STEP
            gate_up_tile(w_ref, t_ref[...], base, half, hidden_total)

        @pl.when(block == 0)
        def _():
            index_table(t_ref, hidden_total)
            total = jnp.sum(x_ref[:, :model_width].astype(jnp.float32), axis=1, keepdims=True)
            shift_ref[...] = jnp.broadcast_to(total * HALF, shift_ref.shape)
            make(0, pre_rows, wa)

        def times(first_row, length, w):
            return jnp.dot(x_ref[:, first_row : first_row + length], w, preferred_element_type=jnp.float32)

        total = times(0, pre_rows, early_ref[0])
        total = total + times(pre_rows, half, wa[...])
        make(block, pre_rows + half, wb)
        total = total + times(pre_rows + half, half, wb[...])
        make(block + 1, pre_rows, wa)
        total = (total - shift_ref[:, :1]) * scale
        gate, up = total[:, :BLOCK], total[:, BLOCK:]
        h_ref[...] = (gate * jax.nn.sigmoid(gate) * up * g_ref[...]).astype(jnp.bfloat16)

    vmem = pl.BlockSpec(memory_space=pltpu.VMEM)
    return pl.pallas_call(
        kernel,
        grid=(blocks,),
        in_specs=[smem(), vmem, vmem, pl.BlockSpec((1, pre_rows, 2 * BLOCK), lambda b: (b, 0, 0))],
        out_specs=pl.BlockSpec((count, BLOCK), lambda b: (0, b)),
        out_shape=jax.ShapeDtypeStruct((count, blocks * BLOCK), jnp.bfloat16),
        scratch_shapes=[
            pltpu.VMEM((16, BLOCK), jnp.int32),
            pltpu.VMEM((half, 2 * BLOCK), jnp.bfloat16),
            pltpu.VMEM((half, 2 * BLOCK), jnp.bfloat16),
            pltpu.VMEM((count, LANES), jnp.float32),
        ],
        compiler_params=params(),
        cost_estimate=estimate(blocks * 2 * half * 2 * BLOCK, count),
        name="hidden_rows",
    )(scalars, rows, row_weight, early)


def early_down(scalars, pre_rows, source_rows, columns, model_width):
    sources = -(-pre_rows // source_rows)

    def kernel(s_ref, w_ref, t_ref):
        index_table(t_ref, model_width)
        column = pl.program_id(0) * wrap(BLOCK * STEP)
        bases = [s_ref[i] + column for i in range(sources)]
        down_tile(w_ref.at[0], t_ref[...], bases, 0, pre_rows, source_rows, model_width)

    return pl.pallas_call(
        kernel,
        grid=(columns // BLOCK,),
        in_specs=[smem()],
        out_specs=pl.BlockSpec((1, pre_rows, BLOCK), lambda b: (b, 0, 0)),
        out_shape=jax.ShapeDtypeStruct((columns // BLOCK, pre_rows, BLOCK), jnp.bfloat16),
        scratch_shapes=[pltpu.VMEM((16, BLOCK), jnp.int32)],
        compiler_params=params(),
        cost_estimate=estimate(columns * pre_rows, 0),
        name="early_down",
    )(scalars)


def output_rows(scalars, hidden, early, source_rows, hidden_total, model_width):
    blocks, pre_rows, _ = early.shape
    count, depth = hidden.shape
    half = (depth - pre_rows) // 2
    sources = depth // source_rows
    scale = math.sqrt(12.0 / hidden_total) / 16777216.0

    def kernel(s_ref, h_ref, early_ref, o_ref, t_ref, wa, wb, shift_ref):
        block = pl.program_id(0)

        def make(step, first_row, w_ref):
            column = step * wrap(BLOCK * STEP)
            bases = [s_ref[i] + column for i in range(sources)]
            down_tile(w_ref, t_ref[...], bases, first_row, half, source_rows, model_width)

        @pl.when(block == 0)
        def _():
            index_table(t_ref, model_width)
            total = jnp.sum(h_ref[...].astype(jnp.float32), axis=1, keepdims=True)
            shift_ref[...] = jnp.broadcast_to(total * HALF, shift_ref.shape)
            make(0, pre_rows, wa)

        def times(first_row, length, w):
            return jnp.dot(h_ref[:, first_row : first_row + length], w, preferred_element_type=jnp.float32)

        total = times(0, pre_rows, early_ref[0])
        total = total + times(pre_rows, half, wa[...])
        make(block, pre_rows + half, wb)
        total = total + times(pre_rows + half, half, wb[...])
        make(block + 1, pre_rows, wa)
        o_ref[...] = ((total - shift_ref[:, :1]) * scale).astype(jnp.bfloat16)

    vmem = pl.BlockSpec(memory_space=pltpu.VMEM)
    return pl.pallas_call(
        kernel,
        grid=(blocks,),
        in_specs=[smem(), vmem, pl.BlockSpec((1, pre_rows, BLOCK), lambda b: (b, 0, 0))],
        out_specs=pl.BlockSpec((count, BLOCK), lambda b: (0, b)),
        out_shape=jax.ShapeDtypeStruct((count, blocks * BLOCK), jnp.bfloat16),
        scratch_shapes=[
            pltpu.VMEM((16, BLOCK), jnp.int32),
            pltpu.VMEM((half, BLOCK), jnp.bfloat16),
            pltpu.VMEM((half, BLOCK), jnp.bfloat16),
            pltpu.VMEM((count, LANES), jnp.float32),
        ],
        compiler_params=params(),
        cost_estimate=estimate(blocks * 2 * half * BLOCK, count),
        name="output_rows",
    )(scalars, hidden, early)


def body(tokens, expert_ids, gate_weights, expert_seeds):
    n_node = lax.axis_size("node")
    n_local = lax.axis_size("local")
    devices = n_node * n_local
    quarters = n_local // EXP_NODE
    quarter_width = FF // quarters
    own_tokens, model_width = tokens.shape
    tok_node = own_tokens * n_local
    capacity = 2 * tok_node * TOP // (EXP_NODE * n_node)
    node_index = lax.axis_index("node")
    local_index = lax.axis_index("local")
    expert_kind = local_index // quarters
    first_unit = (local_index % quarters) * quarter_width
    blocks = quarter_width // BLOCK
    own_seed = expert_seeds[expert_kind]
    up_scalars = jnp.stack([own_seed, first_unit])
    early = early_gate_up(up_scalars, model_width // 2, blocks, FF)

    if devices * own_tokens <= 4 * n_node * capacity:
        pad = LANES - 2 * TOP
        packed = jnp.concatenate(
            [
                tokens,
                expert_ids.astype(jnp.bfloat16),
                gate_weights,
                jnp.zeros((own_tokens, pad), jnp.bfloat16),
            ],
            axis=1,
        )
        every = lax.all_to_all(
            jnp.broadcast_to(packed[None], (devices,) + packed.shape),
            ("node", "local"),
            split_axis=0,
            concat_axis=0,
            tiled=True,
        ).reshape(devices * own_tokens, model_width + LANES)
        routes = every[:, model_width : model_width + 2 * TOP].astype(jnp.float32)
        own_expert = (node_index * EXP_NODE + expert_kind).astype(jnp.float32)
        row_weight = jnp.sum(
            jnp.where(routes[:, :TOP] == own_expert, routes[:, TOP:], 0.0), axis=1, keepdims=True
        )
        hidden = hidden_rows(up_scalars, every, row_weight, early, model_width, FF)
        columns = model_width // n_local
        places = jnp.arange(n_local, dtype=jnp.int32)
        down_scalars = (
            jnp.repeat(expert_seeds, quarters)
            + 2 * CODE
            + ((places % quarters) * quarter_width * model_width + local_index * columns) * STEP
        )
        depth = n_local * quarter_width
        early_low = early_down(down_scalars, depth // 4, quarter_width, columns, model_width)
        shared = lax.all_to_all(
            jnp.broadcast_to(hidden[None], (n_local,) + hidden.shape),
            "local",
            split_axis=0,
            concat_axis=0,
            tiled=True,
        )
        stacked = jnp.transpose(shared, (1, 0, 2)).reshape(hidden.shape[0], depth)
        partial = output_rows(down_scalars, stacked, early_low, quarter_width, FF, model_width)
        returned = lax.all_to_all(
            partial.reshape(devices, own_tokens, columns),
            ("node", "local"),
            split_axis=0,
            concat_axis=0,
            tiled=True,
        )
        summed = jnp.sum(
            returned.reshape(n_node, n_local, own_tokens, columns).astype(jnp.float32), axis=0
        )
        return jnp.transpose(summed, (1, 0, 2)).reshape(own_tokens, model_width).astype(jnp.bfloat16)

    group_rows, group_ids, group_gates = (
        lax.all_gather(tokens, "local", axis=0, tiled=True),
        lax.all_gather(expert_ids, "local", axis=0, tiled=True),
        lax.all_gather(gate_weights, "local", axis=0, tiled=True),
    )
    targets = jnp.arange(n_node, dtype=jnp.int32) * EXP_NODE + expert_kind
    id_match = group_ids[:, :, None] == targets[None, None, :]
    routed = jnp.any(id_match, axis=1)
    picked = jnp.sum(jnp.where(id_match, group_gates.astype(jnp.float32)[:, :, None], 0.0), axis=1)
    place = jnp.where(routed, jnp.cumsum(routed.astype(jnp.int32), axis=0) - 1, -1)
    select = place.T[:, None, :] == jnp.arange(capacity, dtype=jnp.int32)[None, :, None]
    outgoing = jnp.einsum(
        "mct,td->mcd", select.astype(jnp.bfloat16), group_rows, preferred_element_type=jnp.float32
    ).astype(jnp.bfloat16)
    arrived = lax.all_to_all(outgoing, "node", split_axis=0, concat_axis=0, tiled=True)
    flat_rows = arrived.reshape(n_node * capacity, model_width)
    row_weight = jnp.ones((n_node * capacity, 1), jnp.float32)
    hidden = hidden_rows(up_scalars, flat_rows, row_weight, early, model_width, FF)
    down_scalars = (own_seed + 2 * CODE + first_unit * model_width * STEP)[None]
    early_low = early_down(down_scalars, quarter_width // 4, quarter_width, model_width, model_width)
    flat_out = output_rows(down_scalars, hidden, early_low, quarter_width, FF, model_width)
    returned = lax.all_to_all(
        flat_out.reshape(arrived.shape), "node", split_axis=0, concat_axis=0, tiled=True
    )
    combine = select.astype(jnp.float32) * picked.T[:, None, :]
    partial_term = jnp.einsum(
        "mct,mcd->td", combine, returned.astype(jnp.float32), precision=lax.Precision.HIGHEST
    )
    own_rows = lax.psum_scatter(partial_term, "local", scatter_dimension=0, tiled=True)
    return own_rows.astype(jnp.bfloat16)


def solution(mesh):
    return jax.shard_map(
        body,
        mesh=mesh,
        in_specs=(
            P(("node", "local"), None),
            P(("node", "local"), None),
            P(("node", "local"), None),
            P("node"),
        ),
        out_specs=P(("node", "local"), None),
        check_vma=False,
    )
```

time: 203 us -> 132 us (0.65); the launches traced: 199 us -> 131 us
  Pallas kernels: 0 us -> 87.4 us
  other arithmetic: 69.7 us -> 3.5 us
  matrix products: 50.6 us -> 0 us
  blocking collectives: 44.5 us -> 14.8 us
  local copies, waits for them, and re-layouts: 16.9 us -> 8.89 us
  between operations: 2.37 us -> 0.06 us
    pallas_call x0 -> x4, Pallas kernels: none -> 87.4 us  [the longest x1 32.9 us: hidden_rows(): pl.pallas_call(kernel, grid=(blocks,), in_specs=[smem(), vmem, vmem, pl.B...]
    convert_element_type x2, other arithmetic: 69.4 us -> 0.69 us  [the longest x1 0.68 us: body(): expert_ids.astype(jnp.bfloat16)]
    dot_general x18 -> x0, matrix products: 50.6 us -> none  [the longest x8 36.4 us: apply_block(): return jnp.dot(hidden, w_down, preferred_element_type=jnp.float32)]
    all_gather x3 -> x0, blocking collectives: 25.2 us -> none  [the longest x1 10.1 us: body(): lax.all_gather(tokens, 'local', axis=0, tiled=True)]
    unnamed x1 -> x0, blocking collectives: 19.3 us -> none
    all_to_all x0 -> x1, blocking collectives: none -> 14.8 us  [body(): lax.all_to_all(partial.reshape(devices, own_tokens, columns), ('node', 'l...]
    unnamed x34 -> x4, local copies, waits for them, and re-layouts: 12.6 us -> 0.01 us
    broadcast_in_dim x0 -> x4, local copies, waits for them, and re-layouts: none -> 4.36 us  [the longest x1 2.06 us: body(): jnp.broadcast_to(hidden[None], (n_local,) + hidden.shape)]
  transfers between devices with their start and end apart: 2 -> 2, of which waited for: 1 -> 1; matrix products, arithmetic and copies ran while one was open for 36% -> 2% of each run, Pallas kernels for 0% -> 25%
where the time goes in v1:
time: 132 us; the launch traced here: 131 us
  Pallas kernels  87.4 us (66%)
  blocking collectives  14.8 us (11%)
  starting transfers between devices  11.3 us (9%)
  local copies, waits for them, and re-layouts  8.89 us (7%)
  waiting for transfers between devices  5.59 us (4%)
  other arithmetic  3.5 us (3%)
    pallas_call x1, Pallas kernels, hidden_rows(): pl.pallas_call(kernel, grid=(blocks,), in_specs=[smem(), vmem, vmem, pl.B...  32.9 us
    pallas_call x1, Pallas kernels, early_gate_up(): pl.pallas_call(kernel, grid=(blocks, 2), in_specs=[smem()], out_specs=pl....  24.8 us
    pallas_call x1, Pallas kernels, output_rows(): pl.pallas_call(kernel, grid=(blocks,), in_specs=[smem(), vmem, pl.BlockSp...  21.9 us
    all_to_all x1, blocking collectives, body(): lax.all_to_all(partial.reshape(devices, own_tokens, columns), ('node', 'l...  14.8 us
    pallas_call x1, Pallas kernels, early_down(): pl.pallas_call(kernel, grid=(columns // BLOCK,), in_specs=[smem()], out_s...  7.84 us
    all_to_all x1, starting transfers between devices, body(): lax.all_to_all(jnp.broadcast_to(packed[None], (devices,) + packed.shape),...  7.33 us
    all_to_all x1, waiting for transfers between devices, body(): lax.all_to_all(jnp.broadcast_to(hidden[None], (n_local,) + hidden.shape),...  5.59 us
    all_to_all x1, starting transfers between devices, body(): lax.all_to_all(jnp.broadcast_to(hidden[None], (n_local,) + hidden.shape),...  3.94 us
  transfers between devices with their start and end apart: 2, of which 1 were waited for; matrix products, arithmetic and copies ran while one was open for 2% of the time, Pallas kernels for 25%

profile of v1, /device:TPU:0, one launch (start us, length us, event | category | flops | bytes accessed | tf_op | source)
XLA Modules:
  0.0 131.4 jit_solution(12048895628845586203)
XLA Ops:
  0.0 0.7 convert_element_type.24
  0.7 0.8 concatenate.3
  1.5 1.5 %broadcast_in_dim.23 = bf16[32,2,7296]{2,1,0:T(2,128)(2,1)} broadcast(bf16[2,7296]{1,0:T(2,128)(2,1)S(1)} %concatenate.3), dimensions={1,2} | broadcast | bytes 963072 | tf_op jit(solution)/shard_map/broadcast_in_dim | solution.py:244
  3.0 7.3 %all-to-all-start = ((bf16[32,2,7296]{2,1,0:T(2,128)(2,1)}), bf16[32,2,7296]{2,1,0:T(2,128)(2,1)S(1)}, u32[]{:S(2)}, u32[]{:S(2)}) async-start(bf16[32,2,7296]{2,1,0:T(2,128)(2,1)} %broadcast_in_dim.23), calls=%async_computation | async-start | bytes 1867776 | tf_op jit(solution)/shard_map/all_to_all | solution.py:243
  10.4 1.2 dynamic_slice.3
  11.6 1.3 pad_add_fusion.s_ref
  12.9 0.0 copy-start.1
  12.9 24.8 %early_gate_up.1.early_ref = bf16[8,3584,512]{2,1,0:T(8,128)(2,1)} custom-call(s32[2]{0:T(128)} %pad_add_fusion.s_ref), custom_call_target="tpu_custom_call" | custom-call | flops 587202560 | bytes 29360128 | tf_op jit(solution)/shard_map/early_gate_up/pallas_call | solution.py:77
  37.7 0.0 all-to-all-done
  37.7 0.4 reshape.16.x_ref
  38.0 0.0 copy-start
  38.0 0.2 fusion
  38.2 0.8 copy.6.g_ref
  39.0 0.0 copy-done
  39.0 32.9 %hidden_rows.1 = bf16[64,2048]{1,0:T(8,128)(2,1)} custom-call(s32[2]{0:T(128)} %pad_add_fusion.s_ref, bf16[64,7296]{1,0:T(8,128)(2,1)} %copy-done, f32[64,1]{1,0:T(8,128)} %copy.6.g_ref, bf16[8,3584,512]{2,1,0:T(8,128)(2,1)} %early_gate_up.1.early_ref), custom_call_target="tpu_custom_call" | custom-call | flops 2466250752 | bytes 29360128 | tf_op jit(solution)/shard_map/hidden_rows/pallas_call | solution.py:123
  72.0 2.1 %broadcast_in_dim.26 = bf16[4,64,2048]{2,1,0:T(8,128)(2,1)} broadcast(bf16[64,2048]{1,0:T(8,128)(2,1)} %hidden_rows.1), dimensions={1,2} | broadcast | bytes 1310720 | tf_op jit(solution)/shard_map/broadcast_in_dim | solution.py:266
  74.0 3.9 %all-to-all-start.1 = ((bf16[4,64,2048]{2,1,0:T(8,128)(2,1)}), bf16[4,64,2048]{2,1,0:T(8,128)(2,1)S(1)}, u32[]{:S(2)}, u32[]{:S(2)}) async-start(bf16[4,64,2048]{2,1,0:T(8,128)(2,1)} %broadcast_in_dim.26), calls=%async_computation.1 | async-start | bytes 2097152 | tf_op jit(solution)/shard_map/all_to_all | solution.py:265
  78.0 0.0 copy-done.1
  78.0 0.5 add_add_fusion.s_ref
  78.5 7.8 %early_down.1.early_ref = bf16[7,2048,256]{2,1,0:T(8,128)(2,1)} custom-call(s32[4]{0:T(128)} %add_add_fusion.s_ref), custom_call_target="tpu_custom_call" | custom-call | flops 146800640 | bytes 7340032 | tf_op jit(solution)/shard_map/early_down/pallas_call | solution.py:150
  86.3 5.6 %all-to-all-done.1 = bf16[4,64,2048]{2,1,0:T(8,128)(2,1)S(1)} async-done(((bf16[4,64,2048]{2,1,0:T(8,128)(2,1)}), bf16[4,64,2048]{2,1,0:T(8,128)(2,1)S(1)}, u32[]{:S(2)}, u32[]{:S(2)}) %all-to-all-start.1) | async-done | bytes 1048608 | tf_op jit(solution)/shard_map/all_to_all | solution.py:265
  91.9 1.1 copy.8
  93.0 21.9 %output_rows.1 = bf16[64,1792]{1,0:T(8,128)(2,1)} custom-call(s32[4]{0:T(128)} %add_add_fusion.s_ref, bf16[64,8192]{1,0:T(8,128)(2,1)} %bitcast.8, bf16[7,2048,256]{2,1,0:T(8,128)(2,1)} %early_down.1.early_ref), custom_call_target="tpu_custom_call" | custom-call | flops 1849688064 | bytes 22020096 | tf_op jit(solution)/shard_map/output_rows/pallas_call | solution.py:196
  114.8 1.0 reshape.18
  115.9 14.8 %all_to_all.15 = bf16[32,2,1792]{2,1,0:T(2,128)(2,1)S(1)} all-to-all(bf16[32,2,1792]{2,1,0:T(2,128)(2,1)S(1)} %reshape.18), channel_id=1, replica_groups=mesh['node'=8,'local'=4] {'node','local'}, dimensions={0} | all-to-all | bytes 458752 | tf_op jit(solution)/shard_map/all_to_all | solution.py:274
  130.6 0.8 reduce
  (2 shorter events, 0.0 us)
Async XLA Ops:
  3.0 34.6 %all-to-all-start = ((bf16[32,2,7296]{2,1,0:T(2,128)(2,1)}), bf16[32,2,7296]{2,1,0:T(2,128)(2,1)S(1)}, u32[]{:S(2)}, u32[]{:S(2)}) async-start(bf16[32,2,7296]{2,1,0:T(2,128)(2,1)} %broadcast_in_dim.23), calls=%async_computation | async-start | bytes 1867776 | tf_op jit(solution)/shard_map/all_to_all | solution.py:243
  12.9 65.0 %copy-start.1 = (s32[4]{0:T(128)S(1)}, s32[4]{0:T(128)}, u32[]{:S(2)}) copy-start(s32[4]{0:T(128)} %param.7) | copy-start | bytes 52
  38.0 1.0 copy-start
  74.0 17.9 %all-to-all-start.1 = ((bf16[4,64,2048]{2,1,0:T(8,128)(2,1)}), bf16[4,64,2048]{2,1,0:T(8,128)(2,1)S(1)}, u32[]{:S(2)}, u32[]{:S(2)}) async-start(bf16[4,64,2048]{2,1,0:T(8,128)(2,1)} %broadcast_in_dim.26), calls=%async_computation.1 | async-start | bytes 2097152 | tf_op jit(solution)/shard_map/all_to_all | solution.py:265
